TPU v7x, 32 devices: a whole 2x2x4 slice. The times are simulated.
32 devices in a mesh: fsdp: 4 (over y, core), ctx: 4 (over z), tp: 2 (over x).
Axes of the slice: x: 2, y: 2, z: 4, core: 2. Of those that a mesh axis runs over, the one named last changes fastest.
Arguments:
- layer_input: bfloat16 [4, 1024, 1536], P('fsdp', 'ctx'), may hold values from -6 to 6
- segments: int32 [4, 1024], P('fsdp', 'ctx'), may hold values from 0 to 5, as said below
- positions: int32 [4, 1024], P('fsdp', 'ctx'), may hold values from 0 to 1023, as said below
- attn_gain: bfloat16 [1536], P(('fsdp', 'ctx')), may hold values from 0.099609375 to 1.8984375
- query_proj: bfloat16 [1536, 1536], P(('fsdp', 'ctx'), 'tp'), may hold values from -0.21875 to 0.21875
- key_proj: bfloat16 [1536, 768], P(('fsdp', 'ctx'), 'tp'), may hold values from -0.21875 to 0.21875
- value_proj: bfloat16 [1536, 768], P(('fsdp', 'ctx'), 'tp'), may hold values from -0.15625 to 0.15625
- out_proj: bfloat16 [1536, 1536], P('tp', ('fsdp', 'ctx')), may hold values from -1.25 to 1.25
- mlp_gain: bfloat16 [1536], P(('fsdp', 'ctx')), may hold values from 0.099609375 to 1.8984375
- gate_proj: bfloat16 [1536, 4096], P(('fsdp', 'ctx'), 'tp'), may hold values from -0.15625 to 0.15625
- up_proj: bfloat16 [1536, 4096], P(('fsdp', 'ctx'), 'tp'), may hold values from -0.15625 to 0.15625
- down_proj: bfloat16 [4096, 1536], P('tp', ('fsdp', 'ctx')), may hold values from -0.09375 to 0.09375
- out_grad: bfloat16 [4, 1024, 1536], P('fsdp', 'ctx'), may hold values from -6 to 6
Outputs:
- layer_output: bfloat16 [4, 1024, 1536], P('fsdp', 'ctx')
- input_grad: bfloat16 [4, 1024, 1536], P('fsdp', 'ctx')
- attn_gain_grad: float32 [1536], P(('fsdp', 'ctx'))
- query_proj_grad: float32 [1536, 1536], P(('fsdp', 'ctx'), 'tp')
- key_proj_grad: float32 [1536, 768], P(('fsdp', 'ctx'), 'tp')
- value_proj_grad: float32 [1536, 768], P(('fsdp', 'ctx'), 'tp')
- out_proj_grad: float32 [1536, 1536], P('tp', ('fsdp', 'ctx'))
- mlp_gain_grad: float32 [1536], P(('fsdp', 'ctx'))
- gate_proj_grad: float32 [1536, 4096], P(('fsdp', 'ctx'), 'tp')
- up_proj_grad: float32 [1536, 4096], P(('fsdp', 'ctx'), 'tp')
- down_proj_grad: float32 [4096, 1536], P('tp', ('fsdp', 'ctx'))
Inputs may be any that keep to these rules, and one draw needn't show every extreme that they name: `segments`: numbers the documents of each sequence 0, 1, 2 and so on, never falling; every document has 200 to 2000 tokens except that the last of a sequence may be cut short. `positions`: each token's offset from the first token of its document.
All inputs are finite; a program needn't handle non-finite values.
Results may differ from a plain program's by a relative error of at most 0.018.
Values may be sent and summed in bfloat16 or wider, within the bound.
A program may use at most 192 MiB of HBM per device.

v0:
```python
import jax
import jax.numpy as jnp
from jax import lax
from jax.sharding import PartitionSpec as P

HQ = 16
HK = 8
DH = 96
EPS = 1e-05
THETA = 100000.0
NEGATIVE = -1e30


def rotary_tables(positions):
    half_dim = DH // 2
    freq_index = jnp.arange(half_dim, dtype=jnp.float32)
    inverse = THETA ** (-2.0 * freq_index / DH)
    angles = positions.astype(jnp.float32)[..., None] * inverse
    return (jnp.cos(angles), jnp.sin(angles))


def rotate(field_in, cos_table, sin_table):
    half_dim = field_in.shape[-1] // 2
    front_half = field_in[..., :half_dim]
    back_half = field_in[..., half_dim:]
    return jnp.concatenate(
        [
            front_half * cos_table - back_half * sin_table,
            back_half * cos_table + front_half * sin_table,
        ],
        axis=-1,
    )


def unrotate(field_in, cos_table, sin_table):
    half_dim = field_in.shape[-1] // 2
    front_half = field_in[..., :half_dim]
    back_half = field_in[..., half_dim:]
    return jnp.concatenate(
        [
            front_half * cos_table + back_half * sin_table,
            back_half * cos_table - front_half * sin_table,
        ],
        axis=-1,
    )


def inverse_rms(values):
    return lax.rsqrt(jnp.mean(values * values, axis=-1, keepdims=True) + EPS)


def contract(left, right, left_dim, right_dim):
    return lax.dot_general(
        left, right, (((left_dim,), (right_dim,)), ((), ())), preferred_element_type=jnp.float32
    )


def norm_back(upstream, inner, values, scale_rows):
    cubed = scale_rows * scale_rows * scale_rows
    return (
        upstream
        + scale_rows * inner
        - values * cubed * jnp.mean(inner * values, axis=-1, keepdims=True)
    )


def to_blocks(matrix, seq_count, local_kv, groups):
    span = matrix.shape[0] // seq_count
    shaped = matrix.reshape(seq_count, span, local_kv, groups, DH).transpose(0, 2, 1, 3, 4)
    return shaped.reshape(seq_count * local_kv, span * groups, DH)


def from_blocks(blocks, seq_count, local_kv, groups):
    span = blocks.shape[1] // groups
    shaped = blocks.reshape(seq_count, local_kv, span, groups, DH).transpose(0, 2, 1, 3, 4)
    return shaped.reshape(seq_count * span, local_kv * groups * DH)


def seq_items(matrix, local_kv):
    seq_count = matrix.shape[0]
    length = matrix.shape[1]
    return (
        matrix.reshape(seq_count, length, local_kv, DH)
        .transpose(0, 2, 1, 3)
        .reshape(seq_count * local_kv, length, DH)
    )


def from_items(items, seq_count, local_kv):
    length = items.shape[1]
    return (
        items.reshape(seq_count, local_kv, length, DH)
        .transpose(0, 2, 1, 3)
        .reshape(seq_count, length, local_kv * DH)
    )


def on_device(
    layer_input,
    segments,
    positions,
    attn_gain,
    query_proj,
    key_proj,
    value_proj,
    out_proj,
    mlp_gain,
    gate_proj,
    up_proj,
    down_proj,
    out_grad,
):
    attn_full = (
        lax.all_gather(attn_gain, ("fsdp", "ctx"), axis=0, tiled=True),
        lax.all_gather(query_proj, ("fsdp", "ctx"), axis=0, tiled=True),
        lax.all_gather(key_proj, ("fsdp", "ctx"), axis=0, tiled=True),
        lax.all_gather(value_proj, ("fsdp", "ctx"), axis=0, tiled=True),
        lax.all_gather(out_proj, ("fsdp", "ctx"), axis=1, tiled=True),
    )
    mlp_full = (
        lax.all_gather(mlp_gain, ("fsdp", "ctx"), axis=0, tiled=True),
        lax.all_gather(gate_proj, ("fsdp", "ctx"), axis=0, tiled=True),
        lax.all_gather(up_proj, ("fsdp", "ctx"), axis=0, tiled=True),
        lax.all_gather(down_proj, ("fsdp", "ctx"), axis=1, tiled=True),
    )
    seq_count, span, width = layer_input.shape
    total_rows = seq_count * span
    groups = HQ // HK
    local_kv = key_proj.shape[1] // DH
    score_scale = DH ** (-0.5)
    inputs = layer_input.reshape(total_rows, width).astype(jnp.float32)
    scale_attn = inverse_rms(inputs)
    normed_attn = (inputs * scale_attn * attn_full[0].astype(jnp.float32)).astype(jnp.bfloat16)
    query_pre = jnp.dot(normed_attn, attn_full[1], preferred_element_type=jnp.float32)
    key_pre = jnp.dot(normed_attn, attn_full[2], preferred_element_type=jnp.float32)
    value_pre = jnp.dot(normed_attn, attn_full[3], preferred_element_type=jnp.float32)
    cos_table, sin_table = rotary_tables(positions.reshape(total_rows))
    cos_table = cos_table[:, None, :]
    sin_table = sin_table[:, None, :]
    query_rot = (
        rotate(query_pre.reshape(total_rows, -1, DH), cos_table, sin_table)
        .astype(jnp.bfloat16)
        .reshape(total_rows, -1)
    )
    key_rot = (
        rotate(key_pre.reshape(total_rows, local_kv, DH), cos_table, sin_table)
        .astype(jnp.bfloat16)
        .reshape(seq_count, span, local_kv * DH)
    )
    value_low = value_pre.astype(jnp.bfloat16).reshape(seq_count, span, local_kv * DH)
    key_all, value_all, segment_all = (
        lax.all_gather(key_rot, "ctx", axis=1, tiled=True),
        lax.all_gather(value_low, "ctx", axis=1, tiled=True),
        lax.all_gather(segments.astype(jnp.bfloat16), "ctx", axis=1, tiled=True),
    )
    key_items = seq_items(key_all, local_kv)
    value_items = seq_items(value_all, local_kv)
    key_segments = jnp.repeat(segment_all.astype(jnp.int32), local_kv, axis=0)
    query_segments = jnp.repeat(jnp.repeat(segments, groups, axis=1), local_kv, axis=0)
    query_index = jnp.repeat(
        lax.axis_index("ctx") * span + jnp.arange(span, dtype=jnp.int32), groups
    )
    key_index = jnp.arange(key_all.shape[1], dtype=jnp.int32)
    query_blocks = to_blocks(query_rot, seq_count, local_kv, groups)

    def block_scores(block_query, block_keys, key_segment, query_segment):
        scores = (
            jnp.einsum("qd,kd->qk", block_query, block_keys, preferred_element_type=jnp.float32)
            * score_scale
        )
        allowed = (query_segment[:, None] == key_segment[None, :]) & (
            query_index[:, None] >= key_index[None, :]
        )
        return (scores, allowed)

    def forward_block(block_item):
        block_query, block_keys, block_values, key_segment, query_segment = block_item
        scores, allowed = block_scores(block_query, block_keys, key_segment, query_segment)
        scores = jnp.where(allowed, scores, NEGATIVE)
        row_max = jnp.max(scores, axis=1, keepdims=True)
        exp_scores = jnp.exp(scores - row_max)
        row_total = jnp.sum(exp_scores, axis=1, keepdims=True)
        attn_probs = (exp_scores / row_total).astype(jnp.bfloat16)
        mixed_block = jnp.dot(attn_probs, block_values, preferred_element_type=jnp.float32)
        return (mixed_block.astype(jnp.bfloat16), (row_max + jnp.log(row_total))[:, 0])

    mixed_blocks, row_lse = lax.map(
        forward_block, (query_blocks, key_items, value_items, key_segments, query_segments)
    )
    mixed_rows = from_blocks(mixed_blocks, seq_count, local_kv, groups)
    attended = lax.psum(jnp.dot(mixed_rows, attn_full[4], preferred_element_type=jnp.float32), "tp")
    residual = inputs + attended
    scale_mlp = inverse_rms(residual)
    normed_mlp = (residual * scale_mlp * mlp_full[0].astype(jnp.float32)).astype(jnp.bfloat16)
    gate_pre = jnp.dot(normed_mlp, mlp_full[1], preferred_element_type=jnp.float32)
    up_pre = jnp.dot(normed_mlp, mlp_full[2], preferred_element_type=jnp.float32)
    activated = jax.nn.silu(gate_pre)
    hidden = (activated * up_pre).astype(jnp.bfloat16)
    mlp_out = lax.psum(
        jnp.dot(hidden, mlp_full[3], preferred_element_type=jnp.float32).astype(jnp.bfloat16), "tp"
    ).astype(jnp.float32)
    layer_output = (residual + mlp_out).astype(jnp.bfloat16).reshape(seq_count, span, width)
    mlp_back = (
        lax.all_gather(mlp_gain, ("fsdp", "ctx"), axis=0, tiled=True),
        lax.all_gather(gate_proj, ("fsdp", "ctx"), axis=0, tiled=True),
        lax.all_gather(up_proj, ("fsdp", "ctx"), axis=0, tiled=True),
        lax.all_gather(down_proj, ("fsdp", "ctx"), axis=1, tiled=True),
    )
    upstream = out_grad.reshape(total_rows, width).astype(jnp.float32)
    upstream_low = upstream.astype(jnp.bfloat16)
    hidden_grad = contract(upstream_low, mlp_back[3], 1, 1)
    down_weight_grad = contract(hidden, upstream_low, 0, 0)
    sigmoid_gate = jax.nn.sigmoid(gate_pre)
    gate_grad = (
        hidden_grad * up_pre * sigmoid_gate * (1.0 + gate_pre * (1.0 - sigmoid_gate))
    ).astype(jnp.bfloat16)
    up_grad = (hidden_grad * activated).astype(jnp.bfloat16)
    normed_mlp_grad = lax.psum(
        contract(gate_grad, mlp_back[1], 1, 1) + contract(up_grad, mlp_back[2], 1, 1), "tp"
    )
    mlp_gain_term = jnp.sum(normed_mlp_grad * residual * scale_mlp, axis=0)
    residual_grad = norm_back(
        upstream, normed_mlp_grad * mlp_back[0].astype(jnp.float32), residual, scale_mlp
    )
    gate_weight_grad = contract(normed_mlp, gate_grad, 0, 0)
    up_weight_grad = contract(normed_mlp, up_grad, 0, 0)
    mlp_grads = (
        lax.psum_scatter(mlp_gain_term, ("fsdp", "ctx"), scatter_dimension=0, tiled=True),
        lax.psum_scatter(gate_weight_grad, ("fsdp", "ctx"), scatter_dimension=0, tiled=True),
        lax.psum_scatter(up_weight_grad, ("fsdp", "ctx"), scatter_dimension=0, tiled=True),
        lax.psum_scatter(down_weight_grad, ("fsdp", "ctx"), scatter_dimension=1, tiled=True),
    )
    attn_back = (
        lax.all_gather(attn_gain, ("fsdp", "ctx"), axis=0, tiled=True),
        lax.all_gather(query_proj, ("fsdp", "ctx"), axis=0, tiled=True),
        lax.all_gather(key_proj, ("fsdp", "ctx"), axis=0, tiled=True),
        lax.all_gather(value_proj, ("fsdp", "ctx"), axis=0, tiled=True),
        lax.all_gather(out_proj, ("fsdp", "ctx"), axis=1, tiled=True),
    )
    residual_low = residual_grad.astype(jnp.bfloat16)
    out_weight_grad = contract(mixed_rows, residual_low, 0, 0)
    mixed_grad = contract(residual_low, attn_back[4], 1, 1).astype(jnp.bfloat16)
    grad_blocks = to_blocks(mixed_grad, seq_count, local_kv, groups)

    def backward_block(block_item):
        block_query, block_keys, block_values, key_segment, query_segment, block_lse, block_grad = (
            block_item
        )
        scores, allowed = block_scores(block_query, block_keys, key_segment, query_segment)
        attn_probs = jnp.where(allowed, jnp.exp(scores - block_lse[:, None]), 0.0)
        prob_grad = jnp.einsum(
            "qd,kd->qk", block_grad, block_values, preferred_element_type=jnp.float32
        )
        row_delta = jnp.sum(prob_grad * attn_probs, axis=1, keepdims=True)
        score_grad = (attn_probs * (prob_grad - row_delta)).astype(jnp.bfloat16)
        value_grad = jnp.einsum(
            "qk,qd->kd",
            attn_probs.astype(jnp.bfloat16),
            block_grad,
            preferred_element_type=jnp.float32,
        )
        key_grad = (
            jnp.einsum("qk,qd->kd", score_grad, block_query, preferred_element_type=jnp.float32)
            * score_scale
        )
        query_grad = (
            jnp.dot(score_grad, block_keys, preferred_element_type=jnp.float32) * score_scale
        )
        return (query_grad, key_grad, value_grad)

    query_grads, key_grads, value_grads = lax.map(
        backward_block,
        (query_blocks, key_items, value_items, key_segments, query_segments, row_lse, grad_blocks),
    )
    key_back, value_back = (
        lax.psum_scatter(
            from_items(key_grads, seq_count, local_kv).astype(jnp.bfloat16),
            "ctx",
            scatter_dimension=1,
            tiled=True,
        ).astype(jnp.float32),
        lax.psum_scatter(
            from_items(value_grads, seq_count, local_kv).astype(jnp.bfloat16),
            "ctx",
            scatter_dimension=1,
            tiled=True,
        ).astype(jnp.float32),
    )
    query_grad_rows = (
        unrotate(
            from_blocks(query_grads, seq_count, local_kv, groups).reshape(total_rows, -1, DH),
            cos_table,
            sin_table,
        )
        .astype(jnp.bfloat16)
        .reshape(total_rows, -1)
    )
    key_grad_rows = (
        unrotate(key_back.reshape(total_rows, local_kv, DH), cos_table, sin_table)
        .astype(jnp.bfloat16)
        .reshape(total_rows, -1)
    )
    value_grad_rows = value_back.reshape(total_rows, -1).astype(jnp.bfloat16)
    query_weight_grad = contract(normed_attn, query_grad_rows, 0, 0)
    key_weight_grad = contract(normed_attn, key_grad_rows, 0, 0)
    value_weight_grad = contract(normed_attn, value_grad_rows, 0, 0)
    normed_partial = (
        contract(query_grad_rows, attn_back[1], 1, 1)
        + contract(key_grad_rows, attn_back[2], 1, 1)
        + contract(value_grad_rows, attn_back[3], 1, 1)
    )
    normed_attn_grad = lax.psum(normed_partial.astype(jnp.bfloat16), "tp").astype(jnp.float32)
    attn_gain_term = jnp.sum(normed_attn_grad * inputs * scale_attn, axis=0)
    input_grad = norm_back(
        residual_grad, normed_attn_grad * attn_back[0].astype(jnp.float32), inputs, scale_attn
    )
    attn_grads = (
        lax.psum_scatter(attn_gain_term, ("fsdp", "ctx"), scatter_dimension=0, tiled=True),
        lax.psum_scatter(query_weight_grad, ("fsdp", "ctx"), scatter_dimension=0, tiled=True),
        lax.psum_scatter(key_weight_grad, ("fsdp", "ctx"), scatter_dimension=0, tiled=True),
        lax.psum_scatter(value_weight_grad, ("fsdp", "ctx"), scatter_dimension=0, tiled=True),
        lax.psum_scatter(out_weight_grad, ("fsdp", "ctx"), scatter_dimension=1, tiled=True),
    )
    return (
        layer_output,
        input_grad.astype(jnp.bfloat16).reshape(seq_count, span, width),
        attn_grads[0],
        attn_grads[1],
        attn_grads[2],
        attn_grads[3],
        attn_grads[4],
        mlp_grads[0],
        mlp_grads[1],
        mlp_grads[2],
        mlp_grads[3],
    )


def solution(mesh):
    return jax.shard_map(
        on_device,
        mesh=mesh,
        in_specs=(
            P("fsdp", "ctx", None),
            P("fsdp", "ctx"),
            P("fsdp", "ctx"),
            P(("fsdp", "ctx")),
            P(("fsdp", "ctx"), "tp"),
            P(("fsdp", "ctx"), "tp"),
            P(("fsdp", "ctx"), "tp"),
            P("tp", ("fsdp", "ctx")),
            P(("fsdp", "ctx")),
            P(("fsdp", "ctx"), "tp"),
            P(("fsdp", "ctx"), "tp"),
            P("tp", ("fsdp", "ctx")),
            P("fsdp", "ctx", None),
        ),
        out_specs=(
            P("fsdp", "ctx", None),
            P("fsdp", "ctx", None),
            P(("fsdp", "ctx")),
            P(("fsdp", "ctx"), "tp"),
            P(("fsdp", "ctx"), "tp"),
            P(("fsdp", "ctx"), "tp"),
            P("tp", ("fsdp", "ctx")),
            P(("fsdp", "ctx")),
            P(("fsdp", "ctx"), "tp"),
            P(("fsdp", "ctx"), "tp"),
            P("tp", ("fsdp", "ctx")),
        ),
        check_vma=False,
    )
```

profile of v0, /device:TPU:0, one launch (start us, length us, event | category | flops | bytes accessed | tf_op | source)
XLA Modules:
  0.0 1363.1 jit_solution(13727046639164746978)
XLA Ops:
  12.3 12.6 all_gather.45
  28.6 31.5 %all-reduce.5 = (bf16[1536]{0:T(1024)(128)(2,1)S(1)}, bf16[1536]{0:T(1024)(128)(2,1)}) all-reduce(bf16[1536]{0:T(1024)(128)(2,1)S(1)} %dynamic-update-slice, bf16[1536]{0:T(1024)(128)(2,1)S(1)} %dynamic-update-slice.1), channel_id=1, replica_groups=mesh['fsdp'=4,'ctx'=4,'tp'=2] {'fsdp','ctx'}, use_global_device_ids=true, to_apply=%add | all-reduce | flops 3072 | bytes 12288
  64.6 19.5 %all_gather.49 = bf16[1,1024,384]{1,2,0:T(8,128)(2,1)S(1)} all-gather(bf16[1,256,384]{1,2,0:T(8,128)(2,1)S(1)} %bitcast.263), channel_id=1, replica_groups=mesh['fsdp'=4,'ctx'=4,'tp'=2] {'ctx'}, dimensions={1}, use_global_device_ids=true | all-gather | bytes 983040 | tf_op jit(solution)/shard_map/all_gather | solution.py:152
  84.9 7.7 all-gather.13.cloned.1.call-done
  94.4 22.7 %all-gather = bf16[1024,384]{1,0:T(8,128)(2,1)S(1)} all-gather(bf16[256,384]{1,0:T(8,128)(2,1)S(1)} %convolution_convert_fusion.3), channel_id=2, replica_groups=mesh['fsdp'=4,'ctx'=4,'tp'=2] {'ctx'}, dimensions={0}, use_global_device_ids=true | all-gather | bytes 983040 | tf_op jit(solution)/shard_map/all_gather | solution.py:153
  117.6 20.4 %all-gather.9.cloned.1.call-done = bf16[1536,768]{1,0:T(8,128)(2,1)} async-done(((bf16[96,768]{1,0:T(8,128)(2,1)}), bf16[1536,768]{1,0:T(8,128)(2,1)}) %all-gather.9.cloned.1.call-update) | async-done | bytes 2359312 | tf_op jit(solution)/shard_map/all_gather | solution.py:115
  148.3 22.3 %while.28 = (s32[]{:T(128)}, bf16[4,512,96]{1,2,0:T(8,128)(2,1)}, f32[4,512]{1,0:T(4,128)}, s32[4,512]{1,0:T(4,128)}, s32[4,1024]{1,0:T(4,128)}, /*index=5*/bf16...) while((s32[]{:T(128)}, bf16[4,512,96]{1,2,0:T(8,128)(2,1)}, ...), condition=%wide.region_4.5_spmd.clone, body=%wide.region_1.4_spmd.clone.sunk | while | flops 207142400 | bytes 7095425 | solution.py:187
  174.2 7.3 all-gather.15.cloned.1.call-done
  187.4 48.1 %all-reduce.11.cloned.1.call-done = f32[256,1536]{1,0:T(8,128)} async-done(((f32[256,1536]{1,0:T(8,128)}), f32[256,1536]{1,0:T(8,128)}) %all-reduce.11.cloned.1.call-update) | async-done | bytes 1572880 | tf_op jit(solution)/shard_map/psum | solution.py:191
  237.4 62.4 %all-gather.17.cloned.1.call-done = bf16[1536,2048]{1,0:T(8,128)(2,1)} async-done(((bf16[96,2048]{1,0:T(8,128)(2,1)}), bf16[1536,2048]{1,0:T(8,128)(2,1)}) %all-gather.17.cloned.1.call-update) | async-done | bytes 6291472 | tf_op jit(solution)/shard_map/all_gather | solution.py:122
  299.9 6.0 fusion.103
  305.8 57.1 %all-gather.19.cloned.1.call-done = bf16[1536,2048]{1,0:T(8,128)(2,1)} async-done(((bf16[96,2048]{1,0:T(8,128)(2,1)}), bf16[1536,2048]{1,0:T(8,128)(2,1)}) %all-gather.19.cloned.1.call-update) | async-done | bytes 6291472 | tf_op jit(solution)/shard_map/all_gather | solution.py:123
  362.9 5.9 fusion.104
  368.8 57.2 %all-gather.21.cloned.1.call-done = bf16[2048,1536]{0,1:T(8,128)(2,1)} async-done(((bf16[2048,96]{0,1:T(8,128)(2,1)}), bf16[2048,1536]{0,1:T(8,128)(2,1)}) %all-gather.21.cloned.1.call-update) | async-done | bytes 6291472 | tf_op jit(solution)/shard_map/all_gather | solution.py:124
  426.0 7.6 multiply_convert_fusion.1
  433.6 5.4 fusion.105
  442.4 49.9 %all-reduce.13.cloned.1.call-done = f32[256,1536]{1,0:T(8,128)} async-done(((f32[256,1536]{1,0:T(8,128)}), f32[256,1536]{1,0:T(8,128)}) %all-reduce.13.cloned.1.call-update) | async-done | bytes 1572880 | tf_op jit(solution)/shard_map/psum | solution.py:218
  500.8 42.8 %while.29 = (s32[]{:T(128)}, f32[4,512,96]{1,2,0:T(8,128)}, bf16[4,1024,96]{1,2,0:T(8,128)(2,1)}, bf16[4,1024,96]{1,2,0:T(8,128)(2,1)}, s32[4,512]{1,0:T(4,128)}...) while((s32[]{:T(128)}, f32[4,512,96]{1,2,0:T(8,128)}, ...), condition=%wide.region_12.13_spmd.clone, body=%wide.region_10.12_spmd.clone.sunk | while | flops 509754880 | bytes 32221468 | solution.py:271
  544.4 5.8 convolution_convert_fusion.1
  559.8 7.1 reduce-scatter.10.cloned.1.call-done
  572.6 20.0 %reduce-scatter.12.cloned.1.call-done = bf16[1,256,384]{1,2,0:T(8,128)(2,1)} async-done(((bf16[1,1024,384]{1,2,0:T(8,128)(2,1)}), bf16[1,256,384]{1,2,0:T(8,128)(2,1)}) %reduce-scatter.12.cloned.1.call-update) | async-done | bytes 196624 | tf_op jit(solution)/shard_map/reduce_scatter | solution.py:282
  611.7 7.6 fusion.107
  619.4 7.6 fusion.108
  628.2 7.8 fusion.71
  636.6 10.4 all-reduce.15.cloned.1.call-done
  648.7 61.8 %all-reduce.4 = (f32[1536]{0:T(1024)S(1)}, f32[1536]{0:T(1024)S(1)}) all-reduce(f32[1536]{0:T(1024)S(1)} %get-tuple-element.190, f32[1536]{0:T(1024)S(1)} %copy-done.27), channel_id=5, replica_groups=mesh['fsdp'=4,'ctx'=4,'tp'=2] {'fsdp','ctx'}, use_global_device_ids=true, to_apply=%region_18.19.clone | all-reduce | flops 3072 | bytes 24576
  715.1 66.1 %reduce-scatter.18.cloned.1.call-done = f32[96,384]{1,0:T(8,128)} async-done(((f32[1536,384]{1,0:T(8,128)}), f32[96,384]{1,0:T(8,128)}) %reduce-scatter.18.cloned.1.call-update) | async-done | bytes 147472 | tf_op jit(solution)/shard_map/reduce_scatter | solution.py:321
  781.3 79.4 %reduce-scatter.14.cloned.1.call-done = f32[96,768]{1,0:T(8,128)} async-done(((f32[1536,768]{1,0:T(8,128)}), f32[96,768]{1,0:T(8,128)}) %reduce-scatter.14.cloned.1.call-update) | async-done | bytes 294928 | tf_op jit(solution)/shard_map/reduce_scatter | solution.py:319
  860.7 78.9 %reduce-scatter.20.cloned.1.call-done = f32[768,96]{0,1:T(8,128)} async-done(((f32[768,1536]{0,1:T(8,128)}), f32[768,96]{0,1:T(8,128)}) %reduce-scatter.20.cloned.1.call-update) | async-done | bytes 294928 | tf_op jit(solution)/shard_map/reduce_scatter | solution.py:322
  939.6 138.8 %reduce-scatter.22.cloned.1.call-done = f32[96,2048]{1,0:T(8,128)} async-done(((f32[1536,2048]{1,0:T(8,128)}), f32[96,2048]{1,0:T(8,128)}) %reduce-scatter.22.cloned.1.call-update) | async-done | bytes 786448 | tf_op jit(solution)/shard_map/reduce_scatter | solution.py:229
  1078.4 139.0 %reduce-scatter.24.cloned.1.call-done = f32[96,2048]{1,0:T(8,128)} async-done(((f32[1536,2048]{1,0:T(8,128)}), f32[96,2048]{1,0:T(8,128)}) %reduce-scatter.24.cloned.1.call-update) | async-done | bytes 786448 | tf_op jit(solution)/shard_map/reduce_scatter | solution.py:230
  1217.4 139.1 %reduce-scatter.26.cloned.1.call-done = f32[2048,96]{0,1:T(8,128)} async-done(((f32[2048,1536]{0,1:T(8,128)}), f32[2048,96]{0,1:T(8,128)}) %reduce-scatter.26.cloned.1.call-update) | async-done | bytes 786448 | tf_op jit(solution)/shard_map/reduce_scatter | solution.py:231
  (287 shorter events, 156.4 us)
Async XLA Ops:
  7.2 54.9 %copy-start.31 = (s32[1,256]{1,0:T(1,128)S(1)}, s32[1,256]{1,0:T(1,128)}, u32[]{:S(2)}) copy-start(s32[1,256]{1,0:T(1,128)} %param.19) | copy-start | bytes 3076
  7.2 55.2 %all-gather.11.cloned.1.call-start = ((), (), s32[]{:S(2)}) async-start(), calls=%async_computation.10 | async-start | bytes 1253376 | tf_op jit(solution)/shard_map/all_gather | solution.py:116
  7.9 84.6 %all-gather.13.cloned.1.call-start = ((), (), s32[]{:S(2)}) async-start(), calls=%async_computation.11 | async-start | bytes 1253376 | tf_op jit(solution)/shard_map/all_gather | solution.py:117
  8.7 129.4 %all-gather.9.cloned.1.call-start = ((), (), s32[]{:S(2)}) async-start(), calls=%async_computation.9 | async-start | bytes 2506752 | tf_op jit(solution)/shard_map/all_gather | solution.py:115
  9.4 172.0 %all-gather.15.cloned.1.call-start = ((), (), s32[]{:S(2)}) async-start(), calls=%async_computation.12 | async-start | bytes 2506752 | tf_op jit(solution)/shard_map/all_gather | solution.py:118
  10.0 225.6 %all-reduce.11.cloned.1.call-start = ((), (), s32[]{:S(2)}) async-start(), calls=%async_computation.13 | async-start | bytes 3145728 | tf_op jit(solution)/shard_map/psum | solution.py:191
  62.1 80.3 %copy-start.25 = (f32[256]{0:T(256)}, f32[256]{0:T(256)S(1)}, u32[]{:S(2)}) copy-start(f32[256]{0:T(256)S(1)} %get-tuple-element.268) | copy-start | bytes 3076
  62.3 82.6 %copy-start.15 = (f32[256,48]{0,1:T(8,128)}, f32[256,48]{0,1:T(8,128)S(1)}, u32[]{:S(2)}) copy-start(f32[256,48]{0,1:T(8,128)S(1)} %get-tuple-element.265) | copy-start | bytes 147460
  62.3 82.6 %copy-start.17 = (f32[256,48]{0,1:T(8,128)}, f32[256,48]{0,1:T(8,128)S(1)}, u32[]{:S(2)}) copy-start(f32[256,48]{0,1:T(8,128)S(1)} %get-tuple-element.266) | copy-start | bytes 147460
  170.6 14.4 %copy-start.6 = (bf16[4,1024,96]{2,1,0:T(8,128)(2,1)}, bf16[4,1024,96]{2,1,0:T(8,128)(2,1)S(1)}, u32[]{:S(2)}) copy-start(bf16[4,1024,96]{2,1,0:T(8,128)(2,1)S(1)} %get-tuple-element.524) | copy-start | bytes 2359300
  170.6 14.4 %copy-start.7 = (bf16[4,1024,96]{2,1,0:T(8,128)(2,1)}, bf16[4,1024,96]{2,1,0:T(8,128)(2,1)S(1)}, u32[]{:S(2)}) copy-start(bf16[4,1024,96]{2,1,0:T(8,128)(2,1)S(1)} %get-tuple-element.525) | copy-start | bytes 2359300
  174.1 10.9 copy-start.8
  185.1 114.7 %all-gather.17.cloned.1.call-start = ((), (), s32[]{:S(2)}) async-start(), calls=%async_computation.14 | async-start | bytes 6684672 | tf_op jit(solution)/shard_map/all_gather | solution.py:122
  185.7 177.2 %all-gather.19.cloned.1.call-start = ((), (), s32[]{:S(2)}) async-start(), calls=%async_computation.15 | async-start | bytes 6684672 | tf_op jit(solution)/shard_map/all_gather | solution.py:123
  186.4 239.5 %all-gather.21.cloned.1.call-start = ((), (), s32[]{:S(2)}) async-start(), calls=%async_computation.16 | async-start | bytes 6684672 | tf_op jit(solution)/shard_map/all_gather | solution.py:124
  187.2 305.1 %all-reduce.13.cloned.1.call-start = ((), (), s32[]{:S(2)}) async-start(), calls=%async_computation.17 | async-start | bytes 3145728 | tf_op jit(solution)/shard_map/psum | solution.py:218
  433.6 5.4 copy-start.20
  433.6 5.4 copy-start.19
  433.6 5.4 copy-start.32
  442.1 124.8 %reduce-scatter.10.cloned.1.call-start = ((), (), s32[]{:S(2)}) async-start(), calls=%async_computation.18 | async-start | bytes 983040 | tf_op jit(solution)/shard_map/reduce_scatter | solution.py:276
  543.6 49.0 %reduce-scatter.12.cloned.1.call-start = ((), (), s32[]{:S(2)}) async-start(), calls=%async_computation.19 | async-start | bytes 983040 | tf_op jit(solution)/shard_map/reduce_scatter | solution.py:282
  544.4 102.6 %all-reduce.15.cloned.1.call-start = ((), (), s32[]{:S(2)}) async-start(), calls=%async_computation.27 | async-start | bytes 3145728 | tf_op jit(solution)/shard_map/psum | solution.py:199
  596.0 119.2 %reduce-scatter.16.cloned.1.call-start = ((), (), s32[]{:S(2)}) async-start(), calls=%async_computation.21 | async-start | bytes 2506752 | tf_op jit(solution)/shard_map/reduce_scatter | solution.py:320
  599.6 181.6 %reduce-scatter.18.cloned.1.call-start = ((), (), s32[]{:S(2)}) async-start(), calls=%async_computation.22 | async-start | bytes 2506752 | tf_op jit(solution)/shard_map/reduce_scatter | solution.py:321
  602.8 257.9 %reduce-scatter.14.cloned.1.call-start = ((), (), s32[]{:S(2)}) async-start(), calls=%async_computation.20 | async-start | bytes 5013504 | tf_op jit(solution)/shard_map/reduce_scatter | solution.py:319
  605.9 333.7 %reduce-scatter.20.cloned.1.call-start = ((), (), s32[]{:S(2)}) async-start(), calls=%async_computation.23 | async-start | bytes 5013504 | tf_op jit(solution)/shard_map/reduce_scatter | solution.py:322
  611.4 467.1 %reduce-scatter.22.cloned.1.call-start = ((), (), s32[]{:S(2)}) async-start(), calls=%async_computation.24 | async-start | bytes 13369344 | tf_op jit(solution)/shard_map/reduce_scatter | solution.py:229
  619.3 598.1 %reduce-scatter.24.cloned.1.call-start = ((), (), s32[]{:S(2)}) async-start(), calls=%async_computation.25 | async-start | bytes 13369344 | tf_op jit(solution)/shard_map/reduce_scatter | solution.py:230
  627.0 729.6 %reduce-scatter.26.cloned.1.call-start = ((), (), s32[]{:S(2)}) async-start(), calls=%async_computation.26 | async-start | bytes 13369344 | tf_op jit(solution)/shard_map/reduce_scatter | solution.py:231
  635.9 12.7 copy-start.27
  635.9 75.7 %copy-start.29 = (f32[256]{0:T(256)S(1)}, f32[256]{0:T(256)}, u32[]{:S(2)}) copy-start(f32[256]{0:T(256)} %get-tuple-element.267) | copy-start | bytes 3076
  647.0 64.6 %copy-start.12 = (bf16[256,1536]{1,0:T(8,128)(2,1)S(1)}, bf16[256,1536]{1,0:T(8,128)(2,1)}, u32[]{:S(2)}) copy-start(bf16[256,1536]{1,0:T(8,128)(2,1)} %get-tuple-element.239) | copy-start | bytes 2359300
  (35 other events, 72.9 us)
Sparse Core Ops, SparseCore 0:
  10.3 41.3 all-gather.10
  54.0 38.4 all-gather.12
  94.9 43.1 all-gather.8
  140.2 41.1 all-gather.14
  185.2 50.2 all-reduce.10
  238.0 61.8 all-gather.16
  302.4 60.4 all-gather.18
  365.5 60.4 all-gather.20
  442.2 50.0 all-reduce.12
  543.7 23.1 reduce-scatter.9
  569.8 22.7 reduce-scatter.11
  596.1 50.8 all-reduce.14
  651.8 63.2 reduce-scatter.15
  719.3 61.9 reduce-scatter.17
  786.0 74.5 reduce-scatter.13
  865.0 74.5 reduce-scatter.19
  944.6 133.7 reduce-scatter.21
  1083.4 133.9 reduce-scatter.23
  1222.6 133.8 reduce-scatter.25
where the time goes:
time: 1370 us; the launch traced here: 1360 us
  waiting for transfers between devices  994 us (73%)
  blocking collectives  148 us (11%)
  matrix products  127 us (9%)
  local copies, waits for them, and re-layouts  56.2 us (4%)
  other arithmetic  20.3 us (1%)
  between operations  15.7 us (1%)
    reduce_scatter x1, waiting for transfers between devices, on_device(): lax.psum_scatter(down_weight_grad, ('fsdp', 'ctx'), scatter_dimension=1,...  139 us
    reduce_scatter x1, waiting for transfers between devices, on_device(): lax.psum_scatter(up_weight_grad, ('fsdp', 'ctx'), scatter_dimension=0, ti...  139 us
    reduce_scatter x1, waiting for transfers between devices, on_device(): lax.psum_scatter(gate_weight_grad, ('fsdp', 'ctx'), scatter_dimension=0,...  139 us
    unnamed x2, blocking collectives  93.2 us
    reduce_scatter x1, waiting for transfers between devices, on_device(): lax.psum_scatter(query_weight_grad, ('fsdp', 'ctx'), scatter_dimension=0,...  79.4 us
    reduce_scatter x1, waiting for transfers between devices, on_device(): lax.psum_scatter(out_weight_grad, ('fsdp', 'ctx'), scatter_dimension=1, t...  78.9 us
    reduce_scatter x1, waiting for transfers between devices, on_device(): lax.psum_scatter(value_weight_grad, ('fsdp', 'ctx'), scatter_dimension=0,...  66.1 us
    dot_general x14, matrix products, contract(): lax.dot_general(left, right, (((left_dim,), (right_dim,)), ((), ())), pre...  63.5 us
  transfers between devices with their start and end apart: 19, of which 18 were waited for; matrix products, arithmetic and copies ran while one was open for 9% of the time, Pallas kernels for 0%

commit v1 on v0

--- a/solution.py
+++ b/solution.py
@@ -9,6 +9,28 @@
 EPS = 1e-05
 THETA = 100000.0
 NEGATIVE = -1e30
+
+
+def laid_out(pieces, dim):
+    pieces = jnp.moveaxis(pieces, 0, dim)
+    shape = pieces.shape
+    return pieces.reshape(*shape[:dim], shape[dim] * shape[dim + 1], *shape[dim + 2 :])
+
+
+def gather_around(x, axis, dim):
+    size = lax.axis_size(axis)
+    pairs = [(i, (i + 1) % size) for i in range(size)]
+    back = [(b, a) for a, b in pairs]
+    lower, upper = ([], [])
+    for turn in range(size - 1):
+        if turn % 2 == 0:
+            lower.append(lax.ppermute(lower[-1] if lower else x, axis, pairs))
+        else:
+            upper.append(lax.ppermute(upper[-1] if upper else x, axis, back))
+    parts = jnp.stack([*lower[::-1], x, *upper])
+    shift = lax.axis_index(axis) - len(lower)
+    parts = parts[(jnp.arange(size) - shift) % size]
+    return laid_out(parts, dim)
 
 
 def rotary_tables(positions):
@@ -120,7 +142,7 @@
     mlp_full = (
         lax.all_gather(mlp_gain, ("fsdp", "ctx"), axis=0, tiled=True),
         lax.all_gather(gate_proj, ("fsdp", "ctx"), axis=0, tiled=True),
-        lax.all_gather(up_proj, ("fsdp", "ctx"), axis=0, tiled=True),
+        gather_around(up_proj, ("fsdp", "ctx"), 0),
         lax.all_gather(down_proj, ("fsdp", "ctx"), axis=1, tiled=True),
     )
     seq_count, span, width = layer_input.shape

time: 1370 us -> 1410 us (1.029)
  starting transfers between devices: 1.42 us -> 25.7 us
    ppermute x0 -> x15, waiting for transfers between devices: none -> 149 us  [the longest x7 96.5 us: gather_around(): upper.append(lax.ppermute(upper[-1] if upper else x, axis, back))]
    all_gather x1, waiting for transfers between devices: 62.4 us -> 0.02 us  [on_device(): lax.all_gather(gate_proj, ('fsdp', 'ctx'), axis=0, tiled=True)]
    psum x1, waiting for transfers between devices: 48.1 us -> 0.01 us  [on_device(): lax.psum(jnp.dot(mixed_rows, attn_full[4], preferred_element_type=jnp.flo...]
    all_gather x1, waiting for transfers between devices: 57.2 us -> 16.8 us  [on_device(): lax.all_gather(down_proj, ('fsdp', 'ctx'), axis=1, tiled=True)]
    ppermute x0 -> x15, starting transfers between devices: none -> 24.5 us  [the longest x8 14 us: gather_around(): lower.append(lax.ppermute(lower[-1] if lower else x, axis, pairs))]
    unnamed x63 -> x96, local copies, waits for them, and re-layouts: 9.38 us -> 26.9 us
  transfers between devices with their start and end apart: 19 -> 34, of which waited for: 18 -> 29; matrix products, arithmetic and copies ran while one was open for 9% -> 11% of each run, Pallas kernels for 0% -> 0%
where the time goes in v1:
time: 1410 us; the launch traced here: 1400 us
  waiting for transfers between devices  988 us (70%)
  blocking collectives  148 us (10%)
  matrix products  134 us (10%)
  local copies, waits for them, and re-layouts  70.3 us (5%)
  starting transfers between devices  25.7 us (2%)
  other arithmetic  21.6 us (2%)
  between operations  16.1 us (1%)
    reduce_scatter x1, waiting for transfers between devices, on_device(): lax.psum_scatter(down_weight_grad, ('fsdp', 'ctx'), scatter_dimension=1,...  139 us
    reduce_scatter x1, waiting for transfers between devices, on_device(): lax.psum_scatter(gate_weight_grad, ('fsdp', 'ctx'), scatter_dimension=0,...  139 us
    reduce_scatter x1, waiting for transfers between devices, on_device(): lax.psum_scatter(up_weight_grad, ('fsdp', 'ctx'), scatter_dimension=0, ti...  139 us
    unnamed x2, blocking collectives  98.8 us
    ppermute x7, waiting for transfers between devices, gather_around(): upper.append(lax.ppermute(upper[-1] if upper else x, axis, back))  96.5 us
    reduce_scatter x1, waiting for transfers between devices, on_device(): lax.psum_scatter(out_weight_grad, ('fsdp', 'ctx'), scatter_dimension=1, t...  79.4 us
    reduce_scatter x1, waiting for transfers between devices, on_device(): lax.psum_scatter(query_weight_grad, ('fsdp', 'ctx'), scatter_dimension=0,...  78.9 us
    reduce_scatter x1, waiting for transfers between devices, on_device(): lax.psum_scatter(value_weight_grad, ('fsdp', 'ctx'), scatter_dimension=0,...  66.1 us
  transfers between devices with their start and end apart: 34, of which 29 were waited for; matrix products, arithmetic and copies ran while one was open for 11% of the time, Pallas kernels for 0%

profile of v1, /device:TPU:0, one launch (start us, length us, event | category | flops | bytes accessed | tf_op | source)
XLA Modules:
  0.0 1403.6 jit_solution(12557821370029504824)
XLA Ops:
  13.8 37.0 %all-reduce.5 = (bf16[1536]{0:T(1024)(128)(2,1)S(1)}, bf16[1536]{0:T(1024)(128)(2,1)}) all-reduce(bf16[1536]{0:T(1024)(128)(2,1)S(1)} %dynamic-update-slice, bf16[1536]{0:T(1024)(128)(2,1)S(1)} %dynamic-update-slice.1), channel_id=1, replica_groups=mesh['fsdp'=4,'ctx'=4,'tp'=2] {'fsdp','ctx'}, use_global_device_ids=true, to_apply=%add | all-reduce | flops 3072 | bytes 12288
  55.1 7.6 all_gather.44
  65.3 18.8 %all_gather.48 = bf16[1,1024,384]{1,2,0:T(8,128)(2,1)S(1)} all-gather(bf16[1,256,384]{1,2,0:T(8,128)(2,1)S(1)} %bitcast.296), channel_id=1, replica_groups=mesh['fsdp'=4,'ctx'=4,'tp'=2] {'ctx'}, dimensions={1}, use_global_device_ids=true | all-gather | bytes 983040 | tf_op jit(solution)/shard_map/all_gather | solution.py:174
  94.6 22.6 %all-gather = bf16[1024,384]{1,0:T(8,128)(2,1)S(1)} all-gather(bf16[256,384]{1,0:T(8,128)(2,1)S(1)} %convolution_convert_fusion.3), channel_id=2, replica_groups=mesh['fsdp'=4,'ctx'=4,'tp'=2] {'ctx'}, dimensions={0}, use_global_device_ids=true | all-gather | bytes 983040 | tf_op jit(solution)/shard_map/all_gather | solution.py:175
  118.7 19.6 %all-gather.9.cloned.1.call-done = bf16[1536,768]{1,0:T(8,128)(2,1)} async-done(((bf16[96,768]{1,0:T(8,128)(2,1)}), bf16[1536,768]{1,0:T(8,128)(2,1)}) %all-gather.9.cloned.1.call-update) | async-done | bytes 2359312 | tf_op jit(solution)/shard_map/all_gather | solution.py:137
  142.6 24.1 %while.28 = (s32[]{:T(128)}, bf16[4,512,96]{1,2,0:T(8,128)(2,1)}, f32[4,512]{1,0:T(4,128)}, s32[4,512]{1,0:T(4,128)S(1)}, s32[4,1024]{1,0:T(4,128)S(1)}, /*index...) while((s32[]{:T(128)}, bf16[4,512,96]{1,2,0:T(8,128)(2,1)}, ...), condition=%wide.region_4.5_spmd.clone, body=%wide.region_1.4_spmd.clone.sunk | while | flops 207142400 | bytes 7095417 | solution.py:209
  168.5 13.0 all-gather.15.cloned.1.call-done
  187.6 12.6 collective-permute-done
  204.7 9.7 collective-permute-done.1
  222.9 8.4 collective-permute-done.2
  239.8 8.3 collective-permute-done.3
  248.2 26.3 %collective-permute-done.10 = bf16[96,2048]{1,0:T(8,128)(2,1)S(1)} collective-permute-done((bf16[96,2048]{1,0:T(8,128)(2,1)S(1)}, bf16[96,2048]{1,0:T(8,128)(2,1)S(1)}, u32[]{:S(2)}, u32[]{:S(2)}) %collective-permute-start.10) | collective-permute-done | bytes 393248 | tf_op jit(solution)/shard_map/ppermute | solution.py:29
  277.7 21.4 %collective-permute-done.11 = bf16[96,2048]{1,0:T(8,128)(2,1)S(1)} collective-permute-done((bf16[96,2048]{1,0:T(8,128)(2,1)S(1)}, bf16[96,2048]{1,0:T(8,128)(2,1)S(1)}, u32[]{:S(2)}, u32[]{:S(2)}) %collective-permute-start.11) | collective-permute-done | bytes 393248 | tf_op jit(solution)/shard_map/ppermute | solution.py:29
  304.2 10.9 collective-permute-start.6
  315.2 21.5 %collective-permute-done.12 = bf16[96,2048]{1,0:T(8,128)(2,1)} collective-permute-done((bf16[96,2048]{1,0:T(8,128)(2,1)S(1)}, bf16[96,2048]{1,0:T(8,128)(2,1)}, u32[]{:S(2)}, u32[]{:S(2)}) %collective-permute-start.12) | collective-permute-done | bytes 393248 | tf_op jit(solution)/shard_map/ppermute | solution.py:29
  340.1 15.8 %collective-permute-done.13 = bf16[96,2048]{1,0:T(8,128)(2,1)} collective-permute-done((bf16[96,2048]{1,0:T(8,128)(2,1)}, bf16[96,2048]{1,0:T(8,128)(2,1)}, u32[]{:S(2)}, u32[]{:S(2)}) %collective-permute-start.13) | collective-permute-done | bytes 393248 | tf_op jit(solution)/shard_map/ppermute | solution.py:29
  393.1 16.8 %all-gather.19.cloned.1.call-done = bf16[2048,1536]{0,1:T(8,128)(2,1)} async-done(((bf16[2048,96]{0,1:T(8,128)(2,1)}), bf16[2048,1536]{0,1:T(8,128)(2,1)}) %all-gather.19.cloned.1.call-update) | async-done | bytes 6291472 | tf_op jit(solution)/shard_map/all_gather | solution.py:146
  425.7 47.3 %all-gather.21.cloned.1.call-done = bf16[1536,2048]{1,0:T(8,128)(2,1)} async-done(((bf16[96,2048]{1,0:T(8,128)(2,1)}), bf16[1536,2048]{1,0:T(8,128)(2,1)}) %all-gather.21.cloned.1.call-update) | async-done | bytes 6291472 | tf_op jit(solution)/shard_map/all_gather | solution.py:228
  479.7 50.0 %all-reduce.13.cloned.1.call-done = f32[256,1536]{1,0:T(8,128)} async-done(((f32[256,1536]{1,0:T(8,128)}), f32[256,1536]{1,0:T(8,128)}) %all-reduce.13.cloned.1.call-update) | async-done | bytes 1572880 | tf_op jit(solution)/shard_map/psum | solution.py:240
  538.2 45.9 %while.29 = (s32[]{:T(128)}, f32[4,512,96]{1,2,0:T(8,128)}, bf16[4,1024,96]{1,2,0:T(8,128)(2,1)}, bf16[4,1024,96]{1,2,0:T(8,128)(2,1)}, s32[4,512]{1,0:T(4,128)}...) while((s32[]{:T(128)}, f32[4,512,96]{1,2,0:T(8,128)}, ...), condition=%wide.region_12.13_spmd.clone, body=%wide.region_10.12_spmd.clone.sunk | while | flops 509754880 | bytes 25929948 | solution.py:293
  612.0 21.1 %reduce-scatter.12.cloned.1.call-done = bf16[1,256,384]{1,2,0:T(8,128)(2,1)} async-done(((bf16[1,1024,384]{1,2,0:T(8,128)(2,1)}), bf16[1,256,384]{1,2,0:T(8,128)(2,1)}) %reduce-scatter.12.cloned.1.call-update) | async-done | bytes 196624 | tf_op jit(solution)/shard_map/reduce_scatter | solution.py:304
  650.6 7.6 fusion.108
  658.3 7.6 fusion.109
  667.1 7.7 fusion.71
  675.5 12.0 all-reduce.15.cloned.1.call-done
  689.2 61.8 %all-reduce.4 = (f32[1536]{0:T(1024)S(1)}, f32[1536]{0:T(1024)S(1)}) all-reduce(f32[1536]{0:T(1024)S(1)} %get-tuple-element.190, f32[1536]{0:T(1024)S(1)} %copy-done.35), channel_id=5, replica_groups=mesh['fsdp'=4,'ctx'=4,'tp'=2] {'fsdp','ctx'}, use_global_device_ids=true, to_apply=%region_18.19.clone | all-reduce | flops 3072 | bytes 24576
  755.6 66.1 %reduce-scatter.18.cloned.1.call-done = f32[96,384]{1,0:T(8,128)} async-done(((f32[1536,384]{1,0:T(8,128)}), f32[96,384]{1,0:T(8,128)}) %reduce-scatter.18.cloned.1.call-update) | async-done | bytes 147472 | tf_op jit(solution)/shard_map/reduce_scatter | solution.py:343
  821.8 79.4 %reduce-scatter.20.cloned.1.call-done = f32[768,96]{0,1:T(8,128)} async-done(((f32[768,1536]{0,1:T(8,128)}), f32[768,96]{0,1:T(8,128)}) %reduce-scatter.20.cloned.1.call-update) | async-done | bytes 294928 | tf_op jit(solution)/shard_map/reduce_scatter | solution.py:344
  901.2 78.9 %reduce-scatter.14.cloned.1.call-done = f32[96,768]{1,0:T(8,128)} async-done(((f32[1536,768]{1,0:T(8,128)}), f32[96,768]{1,0:T(8,128)}) %reduce-scatter.14.cloned.1.call-update) | async-done | bytes 294928 | tf_op jit(solution)/shard_map/reduce_scatter | solution.py:341
  980.1 138.8 %reduce-scatter.22.cloned.1.call-done = f32[96,2048]{1,0:T(8,128)} async-done(((f32[1536,2048]{1,0:T(8,128)}), f32[96,2048]{1,0:T(8,128)}) %reduce-scatter.22.cloned.1.call-update) | async-done | bytes 786448 | tf_op jit(solution)/shard_map/reduce_scatter | solution.py:251
  1118.9 138.8 %reduce-scatter.24.cloned.1.call-done = f32[96,2048]{1,0:T(8,128)} async-done(((f32[1536,2048]{1,0:T(8,128)}), f32[96,2048]{1,0:T(8,128)}) %reduce-scatter.24.cloned.1.call-update) | async-done | bytes 786448 | tf_op jit(solution)/shard_map/reduce_scatter | solution.py:252
  1257.7 139.1 %reduce-scatter.26.cloned.1.call-done = f32[2048,96]{0,1:T(8,128)} async-done(((f32[2048,1536]{0,1:T(8,128)}), f32[2048,96]{0,1:T(8,128)}) %reduce-scatter.26.cloned.1.call-update) | async-done | bytes 786448 | tf_op jit(solution)/shard_map/reduce_scatter | solution.py:253
  (339 shorter events, 260.6 us)
Async XLA Ops:
  7.2 55.8 %all-gather.11.cloned.1.call-start = ((), (), s32[]{:S(2)}) async-start(), calls=%async_computation.10 | async-start | bytes 1253376 | tf_op jit(solution)/shard_map/all_gather | solution.py:138
  7.9 84.8 %all-gather.13.cloned.1.call-start = ((), (), s32[]{:S(2)}) async-start(), calls=%async_computation.11 | async-start | bytes 1253376 | tf_op jit(solution)/shard_map/all_gather | solution.py:139
  8.7 129.6 %all-gather.9.cloned.1.call-start = ((), (), s32[]{:S(2)}) async-start(), calls=%async_computation.9 | async-start | bytes 2506752 | tf_op jit(solution)/shard_map/all_gather | solution.py:137
  9.4 172.1 %all-gather.15.cloned.1.call-start = ((), (), s32[]{:S(2)}) async-start(), calls=%async_computation.12 | async-start | bytes 2506752 | tf_op jit(solution)/shard_map/all_gather | solution.py:140
  10.0 375.2 %all-reduce.11.cloned.1.call-start = ((), (), s32[]{:S(2)}) async-start(), calls=%async_computation.13 | async-start | bytes 3145728 | tf_op jit(solution)/shard_map/psum | solution.py:213
  185.2 202.0 %all-gather.17.cloned.1.call-start = ((), (), s32[]{:S(2)}) async-start(), calls=%async_computation.14 | async-start | bytes 6684672 | tf_op jit(solution)/shard_map/all_gather | solution.py:144
  185.8 224.1 %all-gather.19.cloned.1.call-start = ((), (), s32[]{:S(2)}) async-start(), calls=%async_computation.15 | async-start | bytes 6684672 | tf_op jit(solution)/shard_map/all_gather | solution.py:146
  186.5 286.4 %all-gather.21.cloned.1.call-start = ((), (), s32[]{:S(2)}) async-start(), calls=%async_computation.16 | async-start | bytes 6684672 | tf_op jit(solution)/shard_map/all_gather | solution.py:228
  200.3 19.1 %collective-permute-start.8 = (bf16[96,2048]{1,0:T(8,128)(2,1)S(1)}, bf16[96,2048]{1,0:T(8,128)(2,1)S(1)}, u32[]{:S(2)}, u32[]{:S(2)}) collective-permute-start(bf16[96,2048]{1,0:T(8,128)(2,1)S(1)} %copy-done.14), channel_id=1, source_target_pairs={{2,0},{4,2},{6,4},{8,6},{10,8},{12,10},{14,12},{16,14},{18,16},{20... | collective-permute-start | bytes 1179656 | tf_op jit(solution)/shard_map/ppermute | solution.py:29
  214.4 16.9 %collective-permute-start.2 = (bf16[96,2048]{1,0:T(8,128)(2,1)S(1)}, bf16[96,2048]{1,0:T(8,128)(2,1)S(1)}, u32[]{:S(2)}, u32[]{:S(2)}) collective-permute-start(bf16[96,2048]{1,0:T(8,128)(2,1)S(1)} %collective-permute-done.1), channel_id=1, source_target_pairs={{0,2},{2,4},{4,6},{6,8},{8,10},{10,12},{12,14},{14,16},{16,18},{18... | collective-permute-start | bytes 1179656 | tf_op jit(solution)/shard_map/ppermute | solution.py:27
  219.4 18.2 %collective-permute-start.9 = (bf16[96,2048]{1,0:T(8,128)(2,1)S(1)}, bf16[96,2048]{1,0:T(8,128)(2,1)S(1)}, u32[]{:S(2)}, u32[]{:S(2)}) collective-permute-start(bf16[96,2048]{1,0:T(8,128)(2,1)S(1)} %collective-permute-done.8), channel_id=1, source_target_pairs={{2,0},{4,2},{6,4},{8,6},{10,8},{12,10},{14,12},{16,14},{18,16},{20... | collective-permute-start | bytes 1179656 | tf_op jit(solution)/shard_map/ppermute | solution.py:29
  231.3 16.9 %collective-permute-start.3 = (bf16[96,2048]{1,0:T(8,128)(2,1)S(1)}, bf16[96,2048]{1,0:T(8,128)(2,1)S(1)}, u32[]{:S(2)}, u32[]{:S(2)}) collective-permute-start(bf16[96,2048]{1,0:T(8,128)(2,1)S(1)} %collective-permute-done.2), channel_id=1, source_target_pairs={{0,2},{2,4},{4,6},{6,8},{8,10},{10,12},{12,14},{14,16},{16,18},{18... | collective-permute-start | bytes 1179656 | tf_op jit(solution)/shard_map/ppermute | solution.py:27
  237.6 36.8 %collective-permute-start.10 = (bf16[96,2048]{1,0:T(8,128)(2,1)S(1)}, bf16[96,2048]{1,0:T(8,128)(2,1)S(1)}, u32[]{:S(2)}, u32[]{:S(2)}) collective-permute-start(bf16[96,2048]{1,0:T(8,128)(2,1)S(1)} %collective-permute-done.9), channel_id=1, source_target_pairs={{2,0},{4,2},{6,4},{8,6},{10,8},{12,10},{14,12},{16,14},{18,16},{20... | collective-permute-start | bytes 1179656 | tf_op jit(solution)/shard_map/ppermute | solution.py:29
  248.2 29.5 %collective-permute-start.4 = (bf16[96,2048]{1,0:T(8,128)(2,1)S(1)}, bf16[96,2048]{1,0:T(8,128)(2,1)S(1)}, u32[]{:S(2)}, u32[]{:S(2)}) collective-permute-start(bf16[96,2048]{1,0:T(8,128)(2,1)S(1)} %collective-permute-done.3), channel_id=1, source_target_pairs={{0,2},{2,4},{4,6},{6,8},{8,10},{10,12},{12,14},{14,16},{16,18},{18... | collective-permute-start | bytes 1179656 | tf_op jit(solution)/shard_map/ppermute | solution.py:27
  274.5 24.6 %collective-permute-start.11 = (bf16[96,2048]{1,0:T(8,128)(2,1)S(1)}, bf16[96,2048]{1,0:T(8,128)(2,1)S(1)}, u32[]{:S(2)}, u32[]{:S(2)}) collective-permute-start(bf16[96,2048]{1,0:T(8,128)(2,1)S(1)} %collective-permute-done.10), channel_id=1, source_target_pairs={{2,0},{4,2},{6,4},{8,6},{10,8},{12,10},{14,12},{16,14},{18,16},{20... | collective-permute-start | bytes 1179656 | tf_op jit(solution)/shard_map/ppermute | solution.py:29
  277.7 26.6 %collective-permute-start.5 = (bf16[96,2048]{1,0:T(8,128)(2,1)S(1)}, bf16[96,2048]{1,0:T(8,128)(2,1)}, u32[]{:S(2)}, u32[]{:S(2)}) collective-permute-start(bf16[96,2048]{1,0:T(8,128)(2,1)S(1)} %collective-permute-done.4), channel_id=1, source_target_pairs={{0,2},{2,4},{4,6},{6,8},{8,10},{10,12},{12,14},{14,16},{16,18},{18... | collective-permute-start | bytes 1179656 | tf_op jit(solution)/shard_map/ppermute | solution.py:27
  299.1 37.6 %collective-permute-start.12 = (bf16[96,2048]{1,0:T(8,128)(2,1)S(1)}, bf16[96,2048]{1,0:T(8,128)(2,1)}, u32[]{:S(2)}, u32[]{:S(2)}) collective-permute-start(bf16[96,2048]{1,0:T(8,128)(2,1)S(1)} %collective-permute-done.11), channel_id=1, source_target_pairs={{2,0},{4,2},{6,4},{8,6},{10,8},{12,10},{14,12},{16,14},{18,16},{20... | collective-permute-start | bytes 1179656 | tf_op jit(solution)/shard_map/ppermute | solution.py:29
  304.2 32.5 %collective-permute-start.6 = (bf16[96,2048]{1,0:T(8,128)(2,1)}, bf16[96,2048]{1,0:T(8,128)(2,1)}, u32[]{:S(2)}, u32[]{:S(2)}) collective-permute-start(bf16[96,2048]{1,0:T(8,128)(2,1)} %collective-permute-done.5), channel_id=1, source_target_pairs={{0,2},{2,4},{4,6},{6,8},{8,10},{10,12},{12,14},{14,16},{16,18},{18... | collective-permute-start | bytes 1179656 | tf_op jit(solution)/shard_map/ppermute | solution.py:27
  315.1 214.6 %all-reduce.13.cloned.1.call-start = ((), (), s32[]{:S(2)}) async-start(), calls=%async_computation.17 | async-start | bytes 3145728 | tf_op jit(solution)/shard_map/psum | solution.py:240
  336.7 19.1 %collective-permute-start.13 = (bf16[96,2048]{1,0:T(8,128)(2,1)}, bf16[96,2048]{1,0:T(8,128)(2,1)}, u32[]{:S(2)}, u32[]{:S(2)}) collective-permute-start(bf16[96,2048]{1,0:T(8,128)(2,1)} %collective-permute-done.12), channel_id=1, source_target_pairs={{2,0},{4,2},{6,4},{8,6},{10,8},{12,10},{14,12},{16,14},{18,16},{20... | collective-permute-start | bytes 1179656 | tf_op jit(solution)/shard_map/ppermute | solution.py:29
  336.7 24.4 %collective-permute-start.7 = (bf16[96,2048]{1,0:T(8,128)(2,1)}, bf16[96,2048]{1,0:T(8,128)(2,1)}, u32[]{:S(2)}, u32[]{:S(2)}) collective-permute-start(bf16[96,2048]{1,0:T(8,128)(2,1)} %collective-permute-done.6), channel_id=1, source_target_pairs={{0,2},{2,4},{4,6},{6,8},{8,10},{10,12},{12,14},{14,16},{16,18},{18... | collective-permute-start | bytes 1179656 | tf_op jit(solution)/shard_map/ppermute | solution.py:27
  355.9 22.1 %collective-permute-start.14 = (bf16[96,2048]{1,0:T(8,128)(2,1)}, bf16[96,2048]{1,0:T(8,128)(2,1)S(1)}, u32[]{:S(2)}, u32[]{:S(2)}) collective-permute-start(bf16[96,2048]{1,0:T(8,128)(2,1)} %collective-permute-done.13), channel_id=1, source_target_pairs={{2,0},{4,2},{6,4},{8,6},{10,8},{12,10},{14,12},{16,14},{18,16},{20... | collective-permute-start | bytes 1179656 | tf_op jit(solution)/shard_map/ppermute | solution.py:29
  479.5 127.9 %reduce-scatter.10.cloned.1.call-start = ((), (), s32[]{:S(2)}) async-start(), calls=%async_computation.18 | async-start | bytes 983040 | tf_op jit(solution)/shard_map/reduce_scatter | solution.py:298
  584.1 49.0 %reduce-scatter.12.cloned.1.call-start = ((), (), s32[]{:S(2)}) async-start(), calls=%async_computation.19 | async-start | bytes 983040 | tf_op jit(solution)/shard_map/reduce_scatter | solution.py:304
  584.9 102.6 %all-reduce.15.cloned.1.call-start = ((), (), s32[]{:S(2)}) async-start(), calls=%async_computation.27 | async-start | bytes 3145728 | tf_op jit(solution)/shard_map/psum | solution.py:221
  636.5 119.1 %reduce-scatter.16.cloned.1.call-start = ((), (), s32[]{:S(2)}) async-start(), calls=%async_computation.21 | async-start | bytes 2506752 | tf_op jit(solution)/shard_map/reduce_scatter | solution.py:342
  638.7 183.1 %reduce-scatter.18.cloned.1.call-start = ((), (), s32[]{:S(2)}) async-start(), calls=%async_computation.22 | async-start | bytes 2506752 | tf_op jit(solution)/shard_map/reduce_scatter | solution.py:343
  641.8 259.4 %reduce-scatter.20.cloned.1.call-start = ((), (), s32[]{:S(2)}) async-start(), calls=%async_computation.23 | async-start | bytes 5013504 | tf_op jit(solution)/shard_map/reduce_scatter | solution.py:344
  646.3 333.8 %reduce-scatter.14.cloned.1.call-start = ((), (), s32[]{:S(2)}) async-start(), calls=%async_computation.20 | async-start | bytes 5013504 | tf_op jit(solution)/shard_map/reduce_scatter | solution.py:341
  650.4 468.6 %reduce-scatter.22.cloned.1.call-start = ((), (), s32[]{:S(2)}) async-start(), calls=%async_computation.24 | async-start | bytes 13369344 | tf_op jit(solution)/shard_map/reduce_scatter | solution.py:251
  658.3 599.4 %reduce-scatter.24.cloned.1.call-start = ((), (), s32[]{:S(2)}) async-start(), calls=%async_computation.25 | async-start | bytes 13369344 | tf_op jit(solution)/shard_map/reduce_scatter | solution.py:252
  666.0 730.9 %reduce-scatter.26.cloned.1.call-start = ((), (), s32[]{:S(2)}) async-start(), calls=%async_computation.26 | async-start | bytes 13369344 | tf_op jit(solution)/shard_map/reduce_scatter | solution.py:253
  (51 other events, 881.9 us)
Sparse Core Ops, SparseCore 0:
  10.3 41.4 all-gather.10
  54.1 38.5 all-gather.12
  95.1 43.1 all-gather.8
  140.4 41.0 all-gather.14
  185.3 50.2 all-reduce.10
  238.0 100.5 all-gather.16
  341.1 68.7 all-gather.18
  412.5 60.4 all-gather.20
  479.6 50.0 all-reduce.12
  584.3 23.1 reduce-scatter.9
  610.3 22.7 reduce-scatter.11
  636.6 50.8 all-reduce.14
  692.3 63.2 reduce-scatter.15
  759.8 61.9 reduce-scatter.17
  826.5 74.6 reduce-scatter.19
  905.5 74.5 reduce-scatter.13
  985.1 133.7 reduce-scatter.21
  1124.0 133.7 reduce-scatter.23
  1262.9 133.8 reduce-scatter.25
